TPU v7x, 32 devices: a whole 2x2x4 slice. The times are simulated.
32 devices in a mesh: parts: 2 (over x), row: 8 (over z, y), col: 2 (over core).
Axes of the slice: x: 2, y: 2, z: 4, core: 2. Of those that a mesh axis runs over, the one named last changes fastest.
Arguments:
- spectra: bfloat16 [4, 32, 2, 32, 1024], P('parts', None, None, ('row', 'col')), parts along dimension 0, may hold values from -6 to 6
- window_flags: int32 [64, 32], P('parts', ('row', 'col')), parts along dimension 0, may hold values 0 or 1
Outputs:
- cross: float32 [4, 2, 2, 16, 32, 1024], P('parts', None, 'col', None, 'row'), parts along dimension 0
There are 2 independent parts, one for each index of `parts`. A program takes and returns all parts, laid end to end along the dimension named above; each array names one. Nothing has to cross between parts.
All inputs are finite; a program needn't handle non-finite values. No bound on the sum of `window_flags` on one device may be relied on, other than what follows from the above.
Results may differ from a plain program's by a relative error of at most 0.0034.
Values may be sent and summed in bfloat16 or wider, within the bound.
A program may use at most 256 MiB of HBM per device.

v0:
```python
import jax
import jax.numpy as jnp
from jax import lax
from jax.sharding import PartitionSpec as P

HALFWIN = 64


epsilon = 1e-06


def window_mean(magnitude):
    bins = magnitude.shape[-1]
    lead = [(0, 0)] * (magnitude.ndim - 1)
    padded = jnp.pad(magnitude, lead + [(HALFWIN + 1, HALFWIN)])
    running = jnp.cumsum(padded, axis=-1)
    total = running[..., 2 * HALFWIN + 1 :] - running[..., :bins]
    positions = jnp.arange(bins, dtype=jnp.int32)
    counted = (
        jnp.minimum(positions + HALFWIN, bins - 1) - jnp.maximum(positions - HALFWIN, 0) + 1
    ).astype(jnp.float32)
    return total / counted


def whiten(values):
    magnitude = jnp.sqrt(values[:, :, 0] * values[:, :, 0] + values[:, :, 1] * values[:, :, 1])
    smooth = window_mean(magnitude)
    return (values / (smooth[:, :, None] + epsilon)).astype(jnp.bfloat16)


def combine_parts(prods, keep):
    real_part = prods[..., 0, 0, :, :, :] + prods[..., 1, 1, :, :, :]
    imag_part = prods[..., 1, 0, :, :, :] - prods[..., 0, 1, :, :, :]
    return jnp.stack([real_part * keep, imag_part * keep], axis=-4)


def on_device(spectra, window_flags):
    per_device = spectra.shape[3]
    flag_values = window_flags.astype(jnp.float32)[None, :, None, :, None]
    payload = whiten(spectra.astype(jnp.float32) * flag_values)
    row_index = lax.axis_index("row")
    col_index = lax.axis_index("col")
    col_count = lax.axis_size("col")
    row_count = lax.axis_size("row")
    half_size = row_count * per_device
    cols_here = col_count * per_device
    slot = jnp.arange(half_size, dtype=jnp.int32)
    first = (slot // per_device * col_count + col_index) * per_device + slot % per_device
    second = row_index * cols_here + jnp.arange(cols_here, dtype=jnp.int32)
    keep = (first[:, None] <= second[None, :]).astype(jnp.float32)[:, :, None]
    pieces = []
    for band_index in range(spectra.shape[0]):
        first_rows = lax.all_gather(payload[band_index : band_index + 1], "row", axis=3, tiled=True)
        second_rows = lax.all_gather(
            payload[band_index : band_index + 1], "col", axis=3, tiled=True
        )
        prods = jnp.einsum(
            "wpif,wqjf->pqijf", first_rows[0], second_rows[0], preferred_element_type=jnp.float32
        )
        pieces.append(combine_parts(prods, keep))
    result = jnp.stack(pieces, axis=0)
    return result[:, :, None]


def solution(mesh):
    in_specs = (P("parts", None, None, ("row", "col"), None), P("parts", ("row", "col")))
    out_specs = P("parts", None, "col", None, "row", None)
    return jax.shard_map(
        on_device, mesh=mesh, in_specs=in_specs, out_specs=out_specs, check_vma=False
    )
```

profile of v0, /device:TPU:25, one launch (start us, length us, event | category | flops | bytes accessed | tf_op | source)
XLA Modules:
  0.0 210.3 jit_solution(13793272223604262475)
XLA Ops:
  6.5 0.7 convert_element_type.26
  7.2 1.3 convert_multiply_fusion
  9.2 36.3 %reduce-window.6 = f32[2,32,2,10,128]{4,3,2,1,0:T(8,128)S(1)} reduce-window(f32[2,32,2,10,128]{4,3,2,1,0:T(8,128)S(1)} %copy.41, f32[]{:T(128)} %constant.44.clone.1), window={size=1x1x1x1x128 pad=0_0x0_0x0_0x0_0x127_0}, to_apply=%region_0.1 | reduce-window | flops 20807680 | bytes 1310724 | tf_op jit(solution)/shard_map/reduce-window
  45.8 0.5 copy.42
  47.1 0.6 fusion.37
  47.8 0.6 divide_convert_fusion
  48.3 0.8 fusion.38
  49.2 0.7 all-gather.3.cloned.1.call-update
  49.9 2.7 %all_gather.14 = bf16[1,32,2,4,1024]{4,1,2,0,3:T(8,128)(2,1)S(1)} all-gather(bf16[1,32,2,2,1024]{4,1,2,0,3:T(8,128)(2,1)} %get-tuple-element.12), channel_id=1, replica_groups=mesh['parts'=2,'row'=8,'col'=2] {'col'}, dimensions={3}, use_global_device_ids=true | all-gather | bytes 786432 | tf_op jit(solution)/shard_map/all_gather | solution.py:54
  52.6 2.6 %copy.52 = bf16[1,32,2,4,1024]{1,3,2,4,0:T(4,128)(2,1)} copy(bf16[1,32,2,4,1024]{4,1,2,0,3:T(8,128)(2,1)S(1)} %all_gather.14) | data formatting | bytes 1048576 | tf_op jit(solution)/shard_map/all_gather | solution.py:54
  55.2 2.4 %all_gather.12 = bf16[1,32,2,4,1024]{4,1,2,0,3:T(8,128)(2,1)S(1)} all-gather(bf16[1,32,2,2,1024]{4,1,2,0,3:T(8,128)(2,1)S(1)} %copy-done), channel_id=1, replica_groups=mesh['parts'=2,'row'=8,'col'=2] {'col'}, dimensions={3}, use_global_device_ids=true | all-gather | bytes 786432 | tf_op jit(solution)/shard_map/all_gather | solution.py:54
  57.6 1.4 copy.46
  59.1 38.3 %all-gather.5.cloned.1.call-done = bf16[1,32,2,16,1024]{4,1,2,0,3:T(8,128)(2,1)} async-done(((bf16[1,32,2,2,1024]{4,1,2,0,3:T(8,128)(2,1)}), bf16[1,32,2,16,1024]{4,1,2,0,3:T(8,128)(2,1)}) %all-gather.5.cloned.1.call-update) | async-done | bytes 2097168 | tf_op jit(solution)/shard_map/all_gather | solution.py:53
  97.4 12.5 %copy.53 = bf16[1,32,2,16,1024]{1,3,2,4,0:T(8,128)(2,1)} copy(bf16[1,32,2,16,1024]{4,1,2,0,3:T(8,128)(2,1)} %all-gather.5.cloned.1.call-done) | data formatting | bytes 4194304 | tf_op jit(solution)/shard_map/all_gather | solution.py:53
  109.9 26.9 %fusion.7 = f32[2,2,16,4,1024]{2,3,4,1,0:T(4,128)} fusion(bf16[1,32,2,16,1024]{1,3,2,4,0:T(8,128)(2,1)} %copy.53, bf16[1,32,2,4,1024]{1,3,2,4,0:T(4,128)(2,1)} %copy.52), kind=kOutput, calls=%fused_computation.5 | convolution fusion | flops 16777216 | bytes 3670016 | tf_op jit(solution)/shard_map/wpif,wqjf->pqijf/dot_general | solution.py:57
  136.7 10.4 %all-gather.3.cloned.1.call-done = bf16[1,32,2,16,1024]{4,1,2,0,3:T(8,128)(2,1)} async-done(((bf16[1,32,2,2,1024]{4,1,2,0,3:T(8,128)(2,1)}), bf16[1,32,2,16,1024]{4,1,2,0,3:T(8,128)(2,1)}) %all-gather.3.cloned.1.call-update) | async-done | bytes 2097168 | tf_op jit(solution)/shard_map/all_gather | solution.py:53
  147.2 12.5 %copy.47 = bf16[1,32,2,16,1024]{1,3,2,4,0:T(8,128)(2,1)} copy(bf16[1,32,2,16,1024]{4,1,2,0,3:T(8,128)(2,1)} %all-gather.3.cloned.1.call-done) | data formatting | bytes 4194304 | tf_op jit(solution)/shard_map/all_gather | solution.py:53
  159.7 26.2 %fusion.4 = f32[2,2,16,4,1024]{2,3,0,1,4:T(4,128)} fusion(bf16[1,32,2,16,1024]{1,3,2,4,0:T(8,128)(2,1)} %copy.47, bf16[1,32,2,4,1024]{1,3,2,4,0:T(4,128)(2,1)S(1)} %copy.46), kind=kOutput, calls=%fused_computation.4 | convolution fusion | flops 16777216 | bytes 3670016 | tf_op jit(solution)/shard_map/wpif,wqjf->pqijf/dot_general | solution.py:57
  185.9 9.5 %fusion.18 = (f32[1,16,4,1024]{1,2,3,0:T(4,128)}, f32[1,16,4,1024]{1,2,3,0:T(4,128)}, f32[1,16,4,1024]{1,2,3,0:T(4,128)S(1)}, f32[1,16,4,1024]{1,2,3,0:T(4,128)}) fusion(f32[2,2,16,4,1024]{2,3,0,1,4:T(4,128)} %fusion.4, f32[16,4]{0,1:T(4,128)S(1)} %compare_convert_fusion, f32[2,2,16,4,1024]{2,3,4,1,0:T(4,128)} %fusion.7), kind=kLoop, calls=%fused_computation.18 | loop fusion | flops 524288 | bytes 3145984 | tf_op jit(solution)/shard_map/mul | solution.py:34
  195.4 1.8 copy.50
  197.2 1.8 copy.51
  199.0 1.8 copy.55
  200.9 0.8 copy.56
  201.8 1.6 copy.57
  (23 shorter events, 2.2 us)
Async XLA Ops:
  6.5 90.8 %all-gather.5.cloned.1.call-start = ((), (), s32[]{:S(2)}) async-start(), calls=%async_computation.1 | async-start | bytes 2359296 | tf_op jit(solution)/shard_map/all_gather | solution.py:53
  46.7 1.0 copy-start.1
  49.2 6.0 %copy-start = (bf16[1,32,2,2,1024]{4,1,2,0,3:T(8,128)(2,1)S(1)}, bf16[1,32,2,2,1024]{4,1,2,0,3:T(8,128)(2,1)}, u32[]{:S(2)}) copy-start(bf16[1,32,2,2,1024]{4,1,2,0,3:T(8,128)(2,1)} %get-tuple-element.11) | copy-start | bytes 786436
  49.2 98.0 %all-gather.3.cloned.1.call-start = ((), (), s32[]{:S(2)}) async-start(), calls=%async_computation | async-start | bytes 2359296 | tf_op jit(solution)/shard_map/all_gather | solution.py:53
Sparse Core Ops, SparseCore 0:
  49.3 48.0 all-gather.4
  99.5 47.6 all-gather.2
where the time goes:
time: 214 us; the launch traced here: 210 us
  matrix products  53.1 us (25%)
  waiting for transfers between devices  49.4 us (23%)
  other arithmetic  49 us (23%)
  local copies, waits for them, and re-layouts  40.1 us (19%)
  between operations  13.5 us (6%)
  blocking collectives  5.05 us (2%)
    dot_general x2, matrix products, on_device(): jnp.einsum('wpif,wqjf->pqijf', first_rows[0], second_rows[0], preferred_e...  53.1 us
    all_gather x2, waiting for transfers between devices, on_device(): lax.all_gather(payload[band_index:band_index + 1], 'row', axis=3, tiled=T...  48.7 us
    another operation x3, other arithmetic  36.6 us
    all_gather x2, local copies, waits for them, and re-layouts, on_device(): lax.all_gather(payload[band_index:band_index + 1], 'row', axis=3, tiled=T...  25 us
    mul x1, other arithmetic, combine_parts(): return jnp.stack([real_part * keep, imag_part * keep], axis=-4)  9.47 us
    mul x4, local copies, waits for them, and re-layouts, combine_parts(): return jnp.stack([real_part * keep, imag_part * keep], axis=-4)  6.3 us
    all_gather x2, blocking collectives, on_device(): lax.all_gather(payload[band_index:band_index + 1], 'col', axis=3, tiled=T...  5.05 us
  transfers between devices with their start and end apart: 2, of which 2 were waited for; matrix products, arithmetic and copies ran while one was open for 21% of the time, Pallas kernels for 0%

commit v1 on v0

--- a/solution.py
+++ b/solution.py
@@ -1,11 +1,14 @@
+import functools
+
 import jax
 import jax.numpy as jnp
 from jax import lax
+from jax.experimental import pallas as pl
+from jax.experimental.pallas import tpu as pltpu
 from jax.sharding import PartitionSpec as P
 
 HALFWIN = 64
-
-
+LANES = 128
 epsilon = 1e-06
 
 
@@ -34,7 +37,7 @@
     return jnp.stack([real_part * keep, imag_part * keep], axis=-4)
 
 
-def on_device(spectra, window_flags):
+def gather_form(spectra, window_flags):
     per_device = spectra.shape[3]
     flag_values = window_flags.astype(jnp.float32)[None, :, None, :, None]
     payload = whiten(spectra.astype(jnp.float32) * flag_values)
@@ -62,7 +65,204 @@
     return result[:, :, None]
 
 
+def whiten_kernel(x_ref, y_ref):
+    bands, chans, _, windows, bins = x_ref.shape
+    step = 2 * LANES
+    chunks = bins // LANES
+    near = lax.broadcasted_iota(jnp.int32, (2 * step, step), 0) - LANES
+    here = lax.broadcasted_iota(jnp.int32, (2 * step, step), 1)
+    inside = (jnp.abs(near - here) <= HALFWIN).astype(jnp.float32).astype(jnp.bfloat16)
+    mags = []
+    for b in range(bands):
+        for c in range(chans):
+            re = x_ref[b, c, 0].astype(jnp.float32)
+            im = x_ref[b, c, 1].astype(jnp.float32)
+            mags.append(jnp.sqrt(re * re + im * im))
+    mag = jnp.concatenate(mags, axis=0)
+    high = mag.astype(jnp.bfloat16)
+    low = (mag - high.astype(jnp.float32)).astype(jnp.bfloat16)
+    for at in range(0, bins, step):
+        start, stop = max(at - LANES, 0), min(at + step + LANES, bins)
+        near_rows = inside[start - at + LANES : stop - at + LANES]
+        total = jnp.dot(
+            high[:, start:stop], near_rows, preferred_element_type=jnp.float32
+        ) + jnp.dot(low[:, start:stop], near_rows, preferred_element_type=jnp.float32)
+        spot = at + lax.broadcasted_iota(jnp.int32, (1, step), 1)
+        counted = (
+            jnp.minimum(spot + HALFWIN, bins - 1) - jnp.maximum(spot - HALFWIN, 0) + 1
+        ).astype(jnp.float32)
+        scale = 1.0 / (total / counted + epsilon)
+        for b in range(bands):
+            for c in range(chans):
+                top = (b * chans + c) * windows
+                for p in range(2):
+                    value = x_ref[b, c, p, :, at : at + step].astype(jnp.float32)
+                    out = (value * scale[top : top + windows]).astype(jnp.bfloat16)
+                    for half in range(2):
+                        y_ref[
+                            b * chunks + at // LANES + half,
+                            pl.ds((c * 2 + p) * windows, windows),
+                        ] = out[:, half * LANES : (half + 1) * LANES]
+
+
+def exchange_kernel(count, cols, x_ref, y_ref, send_sem, recv_sem, own_sem):
+    me = lax.axis_index("row") * cols + lax.axis_index("col")
+    barrier = pltpu.get_barrier_semaphore()
+    for k in range(1, count):
+        peer = lax.rem(me + k, count)
+        pl.semaphore_signal(
+            barrier,
+            inc=1,
+            device_id={"row": peer // cols, "col": lax.rem(peer, cols)},
+            device_id_type=pl.DeviceIdType.MESH,
+        )
+    own = pltpu.make_async_copy(x_ref.at[me], y_ref.at[me], own_sem)
+    own.start()
+    pl.semaphore_wait(barrier, count - 1)
+
+    copies = []
+    for k in range(1, count):
+        peer = lax.rem(me + k, count)
+        copy = pltpu.make_async_remote_copy(
+            src_ref=x_ref.at[peer],
+            dst_ref=y_ref.at[me],
+            send_sem=send_sem.at[k],
+            recv_sem=recv_sem.at[k],
+            device_id={"row": peer // cols, "col": lax.rem(peer, cols)},
+            device_id_type=pl.DeviceIdType.MESH,
+        )
+        copy.start()
+        copies.append(copy)
+    own.wait()
+    for copy in copies:
+        copy.wait()
+
+
+def exchange(x, rows, cols, number):
+    count = rows * cols
+    return pl.pallas_call(
+        functools.partial(exchange_kernel, count, cols),
+        out_shape=jax.ShapeDtypeStruct(x.shape, x.dtype),
+        in_specs=[pl.BlockSpec(memory_space=pl.ANY)],
+        out_specs=pl.BlockSpec(memory_space=pl.ANY),
+        scratch_shapes=[
+            pltpu.SemaphoreType.DMA((count,)),
+            pltpu.SemaphoreType.DMA((count,)),
+            pltpu.SemaphoreType.DMA,
+        ],
+        compiler_params=pltpu.CompilerParams(collective_id=number, has_side_effects=True),
+    )(x)
+
+
+def fold(values):
+    index = lax.broadcasted_iota(jnp.int32, values[0].shape, 0)
+    shift = 1
+    while len(values) > 1:
+        even = lax.rem(index // shift, 2) == 0
+        paired = []
+        for n in range(0, len(values), 2):
+            u, v = values[n], values[n + 1]
+            moved = pltpu.roll(jnp.where(even, v, u), 8 - shift, 0)
+            paired.append(jnp.where(even, u, v) + moved)
+        values = paired
+        shift *= 2
+    return values[0]
+
+
+def by_eight(values):
+    total = values[0:8]
+    for at in range(8, values.shape[0], 8):
+        total = total + values[at : at + 8]
+    return total
+
+
+def cross_kernel(rows, cols, x_ref, o_ref, wide_ref):
+    wide_ref[...] = x_ref[...].astype(jnp.float32)
+    per_row = wide_ref.shape[0] // rows
+
+    @pl.loop(0, rows)
+    def _(r):
+        @pl.loop(0, r + 1)
+        def _(q):
+            for h in range(cols):
+                reals, imags = [], []
+                for k in range(2):
+                    first = q * per_row + h * 2 + k
+                    re_a, im_a = wide_ref[first, 0], wide_ref[first, 1]
+                    for n in range(per_row):
+                        second = r * per_row + n
+                        re_j, im_j = wide_ref[second, 0], wide_ref[second, 1]
+                        reals.append(by_eight(re_a * re_j + im_a * im_j))
+                        imags.append(by_eight(im_a * re_j - re_a * im_j))
+                pair = jnp.concatenate([fold(reals), fold(imags)], axis=0)
+                o_ref[r * cols + h, q] = pair.astype(jnp.bfloat16)
+
+        @pl.loop(r + 1, rows)
+        def _(q):
+            for h in range(cols):
+                o_ref[r * cols + h, q] = jnp.zeros(o_ref.shape[2:], jnp.bfloat16)
+
+
+def place_kernel(bands, x_ref, o_ref):
+    row, col = lax.axis_index("row"), lax.axis_index("col")
+    chunks = x_ref.shape[0] // bands
+    rows = x_ref.shape[1]
+    index = lax.broadcasted_iota(jnp.int32, (8, LANES), 0)
+    second = row * 4 + lax.rem(index, 4)
+    for b in range(bands):
+        for q in range(rows):
+            first = q * 4 + col * 2 + index // 4
+            keep = first <= second
+            for c in range(chunks):
+                pair = x_ref[b * chunks + c, q].astype(jnp.float32)
+                for p in range(2):
+                    value = jnp.where(keep, pair[p * 8 : p * 8 + 8], 0.0)
+                    for k in range(2):
+                        o_ref[b, p, 0, q * 2 + k, :, c * LANES : (c + 1) * LANES] = value[
+                            k * 4 : k * 4 + 4
+                        ]
+
+
+def exchange_form(rows, cols, spectra, window_flags):
+    bands, windows, parts, chans, bins = spectra.shape
+    count = rows * cols
+    flags = jnp.transpose(window_flags).astype(spectra.dtype)[None, :, None, :, None]
+    values = jnp.transpose(spectra, (0, 3, 2, 1, 4)) * flags
+    height = chans * parts * windows
+    payload = pl.pallas_call(
+        whiten_kernel,
+        out_shape=jax.ShapeDtypeStruct((count, height, LANES), jnp.bfloat16),
+    )(values)
+    mine = exchange(payload, rows, cols, 0)
+    mine = mine.reshape(count * chans, parts, windows, LANES)
+    pairs = pl.pallas_call(
+        functools.partial(cross_kernel, rows, cols),
+        out_shape=jax.ShapeDtypeStruct((count, rows, 16, LANES), jnp.bfloat16),
+        scratch_shapes=[pltpu.VMEM(mine.shape, jnp.float32)],
+    )(mine)
+    got = exchange(pairs, rows, cols, 1)
+    return pl.pallas_call(
+        functools.partial(place_kernel, bands),
+        out_shape=jax.ShapeDtypeStruct((bands, 2, 1, rows * chans, cols * chans, bins), jnp.float32),
+    )(got)
+
+
 def solution(mesh):
+    rows, cols = mesh.shape["row"], mesh.shape["col"]
+
+    def on_device(spectra, window_flags):
+        bands, windows, _, chans, bins = spectra.shape
+        fits = (
+            bands * bins == rows * cols * LANES
+            and bins % (2 * LANES) == 0
+            and chans == 2
+            and cols == 2
+            and windows % 16 == 0
+        )
+        if fits:
+            return exchange_form(rows, cols, spectra, window_flags)
+        return gather_form(spectra, window_flags)
+
     in_specs = (P("parts", None, None, ("row", "col"), None), P("parts", ("row", "col")))
     out_specs = P("parts", None, "col", None, "row", None)
     return jax.shard_map(

time: 214 us -> 46.3 us (0.22)
  the two profiles are of different devices: /device:TPU:25 before, /device:TPU:15 now
where the time goes in v1:
time: 46.3 us; the launch traced here: 46 us
  Pallas kernels  43.1 us (93%)
  other arithmetic  2.82 us (6%)
    pallas_call x2, Pallas kernels, exchange(): pl.pallas_call(functools.partial(exchange_kernel, count, cols), out_shape...  33.2 us
    pallas_call x1, Pallas kernels, exchange_form(): pl.pallas_call(functools.partial(cross_kernel, rows, cols), out_shape=jax...  5.36 us
    pallas_call x1, Pallas kernels, exchange_form(): pl.pallas_call(whiten_kernel, out_shape=jax.ShapeDtypeStruct((count, heig...  2.41 us
    pallas_call x1, Pallas kernels, exchange_form(): pl.pallas_call(functools.partial(place_kernel, bands), out_shape=jax.Shap...  2.16 us
    mul x1, other arithmetic, exchange_form(): values = jnp.transpose(spectra, (0, 3, 2, 1, 4)) * flags  2.14 us

profile of v1, /device:TPU:15, one launch (start us, length us, event | category | flops | bytes accessed | tf_op | source)
XLA Modules:
  0.0 46.0 jit_solution(9357151801272848544)
XLA Ops:
  0.0 0.7 %convert_bitcast_fusion = bf16[2,32]{1,0:T(2,128)(2,1)S(1)} fusion(s32[32,2]{0,1:T(2,128)} %param.3), kind=kLoop, calls=%fused_computation.1 | loop fusion | flops 64 | bytes 384 | tf_op jit(solution)/shard_map/convert_element_type | solution.py:229
  0.7 2.1 %bitcast_multiply_fusion.x_ref = bf16[2,2,2,32,1024]{4,3,2,1,0:T(8,128)(2,1)} fusion(bf16[2,32,2,2,1024]{4,3,2,1,0:T(2,128)(2,1)} %param.2, bf16[2,32]{1,0:T(2,128)(2,1)S(1)} %convert_bitcast_fusion), kind=kLoop, calls=%fused_computation | loop fusion | flops 262144 | bytes 1048704 | tf_op jit(solution)/shard_map/mul | solution.py:230
  2.8 2.4 %shard_map.28.x_ref = bf16[16,128,128]{2,1,0:T(8,128)(2,1)} custom-call(bf16[2,2,2,32,1024]{4,3,2,1,0:T(8,128)(2,1)} %bitcast_multiply_fusion.x_ref), custom_call_target="tpu_custom_call" | custom-call | tf_op jit(solution)/shard_map/pallas_call | solution.py:232
  5.2 16.9 %shard_map.29 = bf16[16,128,128]{2,1,0:T(8,128)(2,1)} custom-call(bf16[16,128,128]{2,1,0:T(8,128)(2,1)} %shard_map.28.x_ref), custom_call_target="tpu_custom_call" | custom-call | tf_op jit(solution)/shard_map/pallas_call | solution.py:143
  22.1 5.4 %shard_map.30.x_ref = bf16[16,8,16,128]{3,2,1,0:T(8,128)(2,1)} custom-call(bf16[32,2,32,128]{3,2,1,0:T(8,128)(2,1)} %bitcast.5), custom_call_target="tpu_custom_call" | custom-call | tf_op jit(solution)/shard_map/pallas_call | solution.py:238
  27.5 16.3 %shard_map.31.x_ref = bf16[16,8,16,128]{3,2,1,0:T(8,128)(2,1)} custom-call(bf16[16,8,16,128]{3,2,1,0:T(8,128)(2,1)} %shard_map.30.x_ref), custom_call_target="tpu_custom_call" | custom-call | tf_op jit(solution)/shard_map/pallas_call | solution.py:143
  43.8 2.2 %shard_map.32 = f32[2,2,1,16,4,1024]{5,4,3,2,1,0:T(4,128)} custom-call(bf16[16,8,16,128]{3,2,1,0:T(8,128)(2,1)} %shard_map.31.x_ref), custom_call_target="tpu_custom_call" | custom-call | tf_op jit(solution)/shard_map/pallas_call | solution.py:244

commit v2 on v1

--- a/solution.py
+++ b/solution.py
@@ -65,18 +65,19 @@
     return result[:, :, None]
 
 
-def whiten_kernel(x_ref, y_ref):
-    bands, chans, _, windows, bins = x_ref.shape
+def whiten_windows(x_ref, y_ref, start_window, count_windows):
+    bands, chans, _, _, bins = x_ref.shape
     step = 2 * LANES
     chunks = bins // LANES
     near = lax.broadcasted_iota(jnp.int32, (2 * step, step), 0) - LANES
     here = lax.broadcasted_iota(jnp.int32, (2 * step, step), 1)
     inside = (jnp.abs(near - here) <= HALFWIN).astype(jnp.float32).astype(jnp.bfloat16)
+    picked = pl.ds(start_window, count_windows)
     mags = []
     for b in range(bands):
         for c in range(chans):
-            re = x_ref[b, c, 0].astype(jnp.float32)
-            im = x_ref[b, c, 1].astype(jnp.float32)
+            re = x_ref[b, c, 0, picked].astype(jnp.float32)
+            im = x_ref[b, c, 1, picked].astype(jnp.float32)
             mags.append(jnp.sqrt(re * re + im * im))
     mag = jnp.concatenate(mags, axis=0)
     high = mag.astype(jnp.bfloat16)
@@ -94,64 +95,15 @@
         scale = 1.0 / (total / counted + epsilon)
         for b in range(bands):
             for c in range(chans):
-                top = (b * chans + c) * windows
+                top = (b * chans + c) * count_windows
                 for p in range(2):
-                    value = x_ref[b, c, p, :, at : at + step].astype(jnp.float32)
-                    out = (value * scale[top : top + windows]).astype(jnp.bfloat16)
+                    value = x_ref[b, c, p, picked, at : at + step].astype(jnp.float32)
+                    out = (value * scale[top : top + count_windows]).astype(jnp.bfloat16)
                     for half in range(2):
                         y_ref[
                             b * chunks + at // LANES + half,
-                            pl.ds((c * 2 + p) * windows, windows),
+                            pl.ds((c * 2 + p) * count_windows, count_windows),
                         ] = out[:, half * LANES : (half + 1) * LANES]
-
-
-def exchange_kernel(count, cols, x_ref, y_ref, send_sem, recv_sem, own_sem):
-    me = lax.axis_index("row") * cols + lax.axis_index("col")
-    barrier = pltpu.get_barrier_semaphore()
-    for k in range(1, count):
-        peer = lax.rem(me + k, count)
-        pl.semaphore_signal(
-            barrier,
-            inc=1,
-            device_id={"row": peer // cols, "col": lax.rem(peer, cols)},
-            device_id_type=pl.DeviceIdType.MESH,
-        )
-    own = pltpu.make_async_copy(x_ref.at[me], y_ref.at[me], own_sem)
-    own.start()
-    pl.semaphore_wait(barrier, count - 1)
-
-    copies = []
-    for k in range(1, count):
-        peer = lax.rem(me + k, count)
-        copy = pltpu.make_async_remote_copy(
-            src_ref=x_ref.at[peer],
-            dst_ref=y_ref.at[me],
-            send_sem=send_sem.at[k],
-            recv_sem=recv_sem.at[k],
-            device_id={"row": peer // cols, "col": lax.rem(peer, cols)},
-            device_id_type=pl.DeviceIdType.MESH,
-        )
-        copy.start()
-        copies.append(copy)
-    own.wait()
-    for copy in copies:
-        copy.wait()
-
-
-def exchange(x, rows, cols, number):
-    count = rows * cols
-    return pl.pallas_call(
-        functools.partial(exchange_kernel, count, cols),
-        out_shape=jax.ShapeDtypeStruct(x.shape, x.dtype),
-        in_specs=[pl.BlockSpec(memory_space=pl.ANY)],
-        out_specs=pl.BlockSpec(memory_space=pl.ANY),
-        scratch_shapes=[
-            pltpu.SemaphoreType.DMA((count,)),
-            pltpu.SemaphoreType.DMA((count,)),
-            pltpu.SemaphoreType.DMA,
-        ],
-        compiler_params=pltpu.CompilerParams(collective_id=number, has_side_effects=True),
-    )(x)
 
 
 def fold(values):
@@ -176,31 +128,160 @@
     return total
 
 
-def cross_kernel(rows, cols, x_ref, o_ref, wide_ref):
-    wide_ref[...] = x_ref[...].astype(jnp.float32)
+def cross_row(wide_ref, r, rows, cols, finish):
     per_row = wide_ref.shape[0] // rows
+
+    @pl.loop(0, r + 1)
+    def _(q):
+        for h in range(cols):
+            reals, imags = [], []
+            for k in range(2):
+                first = q * per_row + h * 2 + k
+                re_a, im_a = wide_ref[first, 0], wide_ref[first, 1]
+                for n in range(per_row):
+                    second = r * per_row + n
+                    re_j, im_j = wide_ref[second, 0], wide_ref[second, 1]
+                    reals.append(by_eight(re_a * re_j + im_a * im_j))
+                    imags.append(by_eight(im_a * re_j - re_a * im_j))
+            finish(h, q, jnp.concatenate([fold(reals), fold(imags)], axis=0))
+
+
+def main_kernel(
+    rows, cols, x_ref, got_ref, sent, held, wide_ref, total_ref, pairs,
+    send_sem, recv_sem, own_sem, back_send, back_recv, back_own,
+):
+    count = rows * cols
+    windows = x_ref.shape[3]
+    part_windows = windows // 2
+    row, col = lax.axis_index("row"), lax.axis_index("col")
+    me = row * cols + col
+    order = sorted(range(1, count), key=lambda k: abs(k - count // 2))
+
+    def place_of(peer):
+        return {"row": peer // cols, "col": lax.rem(peer, cols)}
+
+    barrier = pltpu.get_barrier_semaphore()
+    for k in range(1, count):
+        pl.semaphore_signal(
+            barrier,
+            inc=1,
+            device_id=place_of(lax.rem(me + k, count)),
+            device_id_type=pl.DeviceIdType.MESH,
+        )
+    copies, owns = [[], []], []
+    for half in range(2):
+        whiten_windows(x_ref, sent.at[half], half * part_windows, part_windows)
+        if half == 0:
+            pl.semaphore_wait(barrier, count - 1)
+        for k in order:
+            peer = lax.rem(me + k, count)
+            copy = pltpu.make_async_remote_copy(
+                src_ref=sent.at[half, peer],
+                dst_ref=held.at[half, me],
+                send_sem=send_sem.at[half, k],
+                recv_sem=recv_sem.at[half, k],
+                device_id=place_of(peer),
+                device_id_type=pl.DeviceIdType.MESH,
+            )
+            copy.start()
+            copies[half].append(copy)
+        own = pltpu.make_async_copy(sent.at[half, me], held.at[half, me], own_sem.at[half])
+        own.start()
+        owns.append(own)
+
+    def widen(half):
+        owns[half].wait()
+        for copy in copies[half]:
+            copy.wait_recv()
+
+        @pl.loop(0, count)
+        def _(n):
+            for c in range(2):
+                for p in range(2):
+                    wide_ref[n * 2 + c, p] = held[
+                        half, n, pl.ds((c * 2 + p) * part_windows, part_windows)
+                    ].astype(jnp.float32)
+
+    widen(0)
 
     @pl.loop(0, rows)
     def _(r):
-        @pl.loop(0, r + 1)
-        def _(q):
-            for h in range(cols):
-                reals, imags = [], []
-                for k in range(2):
-                    first = q * per_row + h * 2 + k
-                    re_a, im_a = wide_ref[first, 0], wide_ref[first, 1]
-                    for n in range(per_row):
-                        second = r * per_row + n
-                        re_j, im_j = wide_ref[second, 0], wide_ref[second, 1]
-                        reals.append(by_eight(re_a * re_j + im_a * im_j))
-                        imags.append(by_eight(im_a * re_j - re_a * im_j))
-                pair = jnp.concatenate([fold(reals), fold(imags)], axis=0)
-                o_ref[r * cols + h, q] = pair.astype(jnp.bfloat16)
-
-        @pl.loop(r + 1, rows)
-        def _(q):
-            for h in range(cols):
-                o_ref[r * cols + h, q] = jnp.zeros(o_ref.shape[2:], jnp.bfloat16)
+        def keep(h, q, value):
+            total_ref[r * cols + h, q] = value
+
+        cross_row(wide_ref, r, rows, cols, keep)
+
+    widen(1)
+
+    def back_copy(k, h):
+        to = k * cols + h
+        return pltpu.make_async_remote_copy(
+            src_ref=pairs.at[to, pl.ds(0, k + 1)],
+            dst_ref=got_ref.at[me, pl.ds(0, k + 1)],
+            send_sem=back_send.at[to],
+            recv_sem=back_recv.at[me],
+            device_id={"row": k, "col": h},
+            device_id_type=pl.DeviceIdType.MESH,
+        )
+
+    def own_copy(k, h):
+        to = k * cols + h
+        return pltpu.make_async_copy(
+            pairs.at[to, pl.ds(0, k + 1)], got_ref.at[to, pl.ds(0, k + 1)], back_own
+        )
+
+    @pl.loop(0, rows)
+    def _(step):
+        r = lax.rem(row + rows // 2 + step, rows)
+
+        def keep(h, q, value):
+            pairs[r * cols + h, q] = (total_ref[r * cols + h, q] + value).astype(jnp.bfloat16)
+
+        cross_row(wide_ref, r, rows, cols, keep)
+        for k in range(rows):
+
+            @pl.when(r == k)
+            def _():
+                for h in range(cols):
+
+                    @pl.when(me != k * cols + h)
+                    def _():
+                        back_copy(k, h).start()
+
+                    @pl.when(me == k * cols + h)
+                    def _():
+                        own_copy(k, h).start()
+
+    for half in range(2):
+        for copy in copies[half]:
+            copy.wait_send()
+    for k in range(rows):
+        for h in range(cols):
+
+            @pl.when(me != k * cols + h)
+            def _():
+                back_copy(k, h).wait_send()
+
+    for k in range(rows):
+
+        @pl.when(row == k)
+        def _():
+            for n in range(count):
+
+                @pl.when(me != n)
+                def _():
+                    pltpu.make_async_remote_copy(
+                        src_ref=pairs.at[0, pl.ds(0, k + 1)],
+                        dst_ref=got_ref.at[n, pl.ds(0, k + 1)],
+                        send_sem=back_send.at[n],
+                        recv_sem=back_recv.at[n],
+                        device_id={"row": n // cols, "col": n % cols},
+                        device_id_type=pl.DeviceIdType.MESH,
+                    ).wait_recv()
+
+                @pl.when(me == n)
+                def _():
+                    own_copy(k, n % cols).wait()
 
 
 def place_kernel(bands, x_ref, o_ref):
@@ -229,18 +310,26 @@
     flags = jnp.transpose(window_flags).astype(spectra.dtype)[None, :, None, :, None]
     values = jnp.transpose(spectra, (0, 3, 2, 1, 4)) * flags
     height = chans * parts * windows
-    payload = pl.pallas_call(
-        whiten_kernel,
-        out_shape=jax.ShapeDtypeStruct((count, height, LANES), jnp.bfloat16),
+    got = pl.pallas_call(
+        functools.partial(main_kernel, rows, cols),
+        out_shape=jax.ShapeDtypeStruct((count, rows, 16, LANES), jnp.bfloat16),
+        in_specs=[pl.BlockSpec(memory_space=pltpu.VMEM)],
+        out_specs=pl.BlockSpec(memory_space=pl.ANY),
+        scratch_shapes=[
+            pltpu.VMEM((2, count, height // 2, LANES), jnp.bfloat16),
+            pltpu.VMEM((2, count, height // 2, LANES), jnp.bfloat16),
+            pltpu.VMEM((count * chans, parts, windows // 2, LANES), jnp.float32),
+            pltpu.VMEM((count, rows, 16, LANES), jnp.float32),
+            pltpu.VMEM((count, rows, 16, LANES), jnp.bfloat16),
+            pltpu.SemaphoreType.DMA((2, count)),
+            pltpu.SemaphoreType.DMA((2, count)),
+            pltpu.SemaphoreType.DMA((2,)),
+            pltpu.SemaphoreType.DMA((count,)),
+            pltpu.SemaphoreType.DMA((count,)),
+            pltpu.SemaphoreType.DMA,
+        ],
+        compiler_params=pltpu.CompilerParams(collective_id=0, has_side_effects=True),
     )(values)
-    mine = exchange(payload, rows, cols, 0)
-    mine = mine.reshape(count * chans, parts, windows, LANES)
-    pairs = pl.pallas_call(
-        functools.partial(cross_kernel, rows, cols),
-        out_shape=jax.ShapeDtypeStruct((count, rows, 16, LANES), jnp.bfloat16),
-        scratch_shapes=[pltpu.VMEM(mine.shape, jnp.float32)],
-    )(mine)
-    got = exchange(pairs, rows, cols, 1)
     return pl.pallas_call(
         functools.partial(place_kernel, bands),
         out_shape=jax.ShapeDtypeStruct((bands, 2, 1, rows * chans, cols * chans, bins), jnp.float32),
@@ -257,7 +346,7 @@
             and bins % (2 * LANES) == 0
             and chans == 2
             and cols == 2
-            and windows % 16 == 0
+            and windows % 32 == 0
         )
         if fits:
             return exchange_form(rows, cols, spectra, window_flags)

time: 46.3 us -> 34.8 us (0.75)
  the two profiles are of different devices: /device:TPU:15 before, /device:TPU:25 now
where the time goes in v2:
time: 34.8 us; the launch traced here: 34.6 us
  Pallas kernels  31.7 us (91%)
  other arithmetic  2.82 us (8%)
    pallas_call x1, Pallas kernels, exchange_form(): pl.pallas_call(functools.partial(main_kernel, rows, cols), out_shape=jax....  29.6 us
    pallas_call x1, Pallas kernels, exchange_form(): pl.pallas_call(functools.partial(place_kernel, bands), out_shape=jax.Shap...  2.16 us
    mul x1, other arithmetic, exchange_form(): values = jnp.transpose(spectra, (0, 3, 2, 1, 4)) * flags  2.14 us

profile of v2, /device:TPU:25, one launch (start us, length us, event | category | flops | bytes accessed | tf_op | source)
XLA Modules:
  0.0 34.6 jit_solution(18411784376778602950)
XLA Ops:
  0.0 0.7 %convert_bitcast_fusion = bf16[2,32]{1,0:T(2,128)(2,1)S(1)} fusion(s32[32,2]{0,1:T(2,128)} %param.3), kind=kLoop, calls=%fused_computation.1 | loop fusion | flops 64 | bytes 384 | tf_op jit(solution)/shard_map/convert_element_type | solution.py:310
  0.7 2.1 %bitcast_multiply_fusion.x_ref = bf16[2,2,2,32,1024]{4,3,2,1,0:T(8,128)(2,1)} fusion(bf16[2,32,2,2,1024]{4,3,2,1,0:T(2,128)(2,1)} %param.2, bf16[2,32]{1,0:T(2,128)(2,1)S(1)} %convert_bitcast_fusion), kind=kLoop, calls=%fused_computation | loop fusion | flops 262144 | bytes 1048704 | tf_op jit(solution)/shard_map/mul | solution.py:311
  2.8 29.6 %shard_map.28.x_ref = bf16[16,8,16,128]{3,2,1,0:T(8,128)(2,1)} custom-call(bf16[2,2,2,32,1024]{4,3,2,1,0:T(8,128)(2,1)} %bitcast_multiply_fusion.x_ref), custom_call_target="tpu_custom_call" | custom-call | tf_op jit(solution)/shard_map/pallas_call | solution.py:313
  32.4 2.2 %shard_map.29 = f32[2,2,1,16,4,1024]{5,4,3,2,1,0:T(4,128)} custom-call(bf16[16,8,16,128]{3,2,1,0:T(8,128)(2,1)} %shard_map.28.x_ref), custom_call_target="tpu_custom_call" | custom-call | tf_op jit(solution)/shard_map/pallas_call | solution.py:333

commit v3 on v2

--- a/solution.py
+++ b/solution.py
@@ -65,20 +65,42 @@
     return result[:, :, None]
 
 
-def whiten_windows(x_ref, y_ref, start_window, count_windows):
-    bands, chans, _, _, bins = x_ref.shape
+def spread_windows(x_ref, flag_ref, rows_ref, start_window, count_windows):
+    bands, _, parts, chans, _ = x_ref.shape
+    for b in range(bands):
+        for w in range(count_windows):
+            for p in range(parts):
+                pair = x_ref[b, start_window + w, p].astype(jnp.float32)
+                for n in range(rows_ref.shape[2]):
+                    rows_ref[b, p, n, pl.ds(w * chans, chans)] = pair[:, n * LANES : (n + 1) * LANES]
+    extent = (count_windows, flag_ref.shape[1])
+    here = lax.broadcasted_iota(jnp.int32, extent, 0) + start_window
+    same = here == lax.broadcasted_iota(jnp.int32, extent, 1)
+    flags = flag_ref[...].astype(jnp.float32)
+    return [
+        jnp.sum(jnp.where(same, flags[c : c + 1], 0.0), axis=1, keepdims=True)
+        for c in range(chans)
+    ]
+
+
+def whiten_windows(x_ref, flag_ref, rows_ref, y_ref, start_window, count_windows):
+    bands, _, _, chans, bins = x_ref.shape
+    flags = spread_windows(x_ref, flag_ref, rows_ref, start_window, count_windows)
     step = 2 * LANES
     chunks = bins // LANES
     near = lax.broadcasted_iota(jnp.int32, (2 * step, step), 0) - LANES
     here = lax.broadcasted_iota(jnp.int32, (2 * step, step), 1)
     inside = (jnp.abs(near - here) <= HALFWIN).astype(jnp.float32).astype(jnp.bfloat16)
-    picked = pl.ds(start_window, count_windows)
     mags = []
     for b in range(bands):
         for c in range(chans):
-            re = x_ref[b, c, 0, picked].astype(jnp.float32)
-            im = x_ref[b, c, 1, picked].astype(jnp.float32)
-            mags.append(jnp.sqrt(re * re + im * im))
+            picked = pl.ds(c, count_windows, stride=chans)
+            line = []
+            for n in range(chunks):
+                re = rows_ref[b, 0, n, picked] * flags[c]
+                im = rows_ref[b, 1, n, picked] * flags[c]
+                line.append(jnp.sqrt(re * re + im * im))
+            mags.append(jnp.concatenate(line, axis=1))
     mag = jnp.concatenate(mags, axis=0)
     high = mag.astype(jnp.bfloat16)
     low = (mag - high.astype(jnp.float32)).astype(jnp.bfloat16)
@@ -96,14 +118,16 @@
         for b in range(bands):
             for c in range(chans):
                 top = (b * chans + c) * count_windows
+                picked = pl.ds(c, count_windows, stride=chans)
                 for p in range(2):
-                    value = x_ref[b, c, p, picked, at : at + step].astype(jnp.float32)
-                    out = (value * scale[top : top + count_windows]).astype(jnp.bfloat16)
                     for half in range(2):
+                        lanes = slice(half * LANES, (half + 1) * LANES)
+                        value = rows_ref[b, p, at // LANES + half, picked] * flags[c]
+                        out = value * scale[top : top + count_windows, lanes]
                         y_ref[
                             b * chunks + at // LANES + half,
                             pl.ds((c * 2 + p) * count_windows, count_windows),
-                        ] = out[:, half * LANES : (half + 1) * LANES]
+                        ] = out.astype(jnp.bfloat16)
 
 
 def fold(values):
@@ -147,11 +171,11 @@
 
 
 def main_kernel(
-    rows, cols, x_ref, got_ref, sent, held, wide_ref, total_ref, pairs,
+    rows, cols, x_ref, flag_ref, got_ref, spread, sent, held, wide_ref, total_ref, pairs,
     send_sem, recv_sem, own_sem, back_send, back_recv, back_own,
 ):
     count = rows * cols
-    windows = x_ref.shape[3]
+    windows = x_ref.shape[1]
     part_windows = windows // 2
     row, col = lax.axis_index("row"), lax.axis_index("col")
     me = row * cols + col
@@ -170,7 +194,7 @@
         )
     copies, owns = [[], []], []
     for half in range(2):
-        whiten_windows(x_ref, sent.at[half], half * part_windows, part_windows)
+        whiten_windows(x_ref, flag_ref, spread, sent.at[half], half * part_windows, part_windows)
         if half == 0:
             pl.semaphore_wait(barrier, count - 1)
         for k in order:
@@ -284,38 +308,34 @@
                     own_copy(k, n % cols).wait()
 
 
-def place_kernel(bands, x_ref, o_ref):
+def place_kernel(x_ref, o_ref):
     row, col = lax.axis_index("row"), lax.axis_index("col")
-    chunks = x_ref.shape[0] // bands
-    rows = x_ref.shape[1]
+    chunks, rows = x_ref.shape[:2]
     index = lax.broadcasted_iota(jnp.int32, (8, LANES), 0)
     second = row * 4 + lax.rem(index, 4)
-    for b in range(bands):
-        for q in range(rows):
-            first = q * 4 + col * 2 + index // 4
-            keep = first <= second
-            for c in range(chunks):
-                pair = x_ref[b * chunks + c, q].astype(jnp.float32)
-                for p in range(2):
-                    value = jnp.where(keep, pair[p * 8 : p * 8 + 8], 0.0)
-                    for k in range(2):
-                        o_ref[b, p, 0, q * 2 + k, :, c * LANES : (c + 1) * LANES] = value[
-                            k * 4 : k * 4 + 4
-                        ]
+    for q in range(rows):
+        keep = q * 4 + col * 2 + index // 4 <= second
+        for c in range(chunks):
+            pair = x_ref[c, q].astype(jnp.float32)
+            for p in range(2):
+                value = jnp.where(keep, pair[p * 8 : p * 8 + 8], 0.0)
+                for k in range(2):
+                    o_ref[0, p, 0, q * 2 + k, :, c * LANES : (c + 1) * LANES] = value[
+                        k * 4 : k * 4 + 4
+                    ]
 
 
 def exchange_form(rows, cols, spectra, window_flags):
     bands, windows, parts, chans, bins = spectra.shape
     count = rows * cols
-    flags = jnp.transpose(window_flags).astype(spectra.dtype)[None, :, None, :, None]
-    values = jnp.transpose(spectra, (0, 3, 2, 1, 4)) * flags
     height = chans * parts * windows
     got = pl.pallas_call(
         functools.partial(main_kernel, rows, cols),
         out_shape=jax.ShapeDtypeStruct((count, rows, 16, LANES), jnp.bfloat16),
-        in_specs=[pl.BlockSpec(memory_space=pltpu.VMEM)],
+        in_specs=[pl.BlockSpec(memory_space=pltpu.VMEM)] * 2,
         out_specs=pl.BlockSpec(memory_space=pl.ANY),
         scratch_shapes=[
+            pltpu.VMEM((bands, parts, bins // LANES, windows // 2 * chans, LANES), jnp.float32),
             pltpu.VMEM((2, count, height // 2, LANES), jnp.bfloat16),
             pltpu.VMEM((2, count, height // 2, LANES), jnp.bfloat16),
             pltpu.VMEM((count * chans, parts, windows // 2, LANES), jnp.float32),
@@ -329,9 +349,15 @@
             pltpu.SemaphoreType.DMA,
         ],
         compiler_params=pltpu.CompilerParams(collective_id=0, has_side_effects=True),
-    )(values)
+    )(spectra, jnp.transpose(window_flags))
+    chunks = count // bands // 2
     return pl.pallas_call(
-        functools.partial(place_kernel, bands),
+        place_kernel,
+        grid=(bands, 2),
+        in_specs=[pl.BlockSpec((chunks, rows, 16, LANES), lambda b, n: (b * 2 + n, 0, 0, 0))],
+        out_specs=pl.BlockSpec(
+            (1, 2, 1, rows * chans, cols * chans, bins // 2), lambda b, n: (b, 0, 0, 0, 0, n)
+        ),
         out_shape=jax.ShapeDtypeStruct((bands, 2, 1, rows * chans, cols * chans, bins), jnp.float32),
     )(got)
 

time: 34.8 us -> 33.1 us (0.951)
  other arithmetic: 2.82 us -> 0 us
  Pallas kernels: 31.7 us -> 32.9 us
    mul x1 -> x0, other arithmetic: 2.14 us -> none  [exchange_form(): values = jnp.transpose(spectra, (0, 3, 2, 1, 4)) * flags]
    pallas_call x1, Pallas kernels: 2.16 us -> 3.33 us  [exchange_form(): pl.pallas_call(place_kernel, grid=(bands, 2), in_specs=[pl.BlockSpec((chu...]
    convert_element_type x1 -> x0, other arithmetic: 0.68 us -> none  [exchange_form(): jnp.transpose(window_flags).astype(spectra.dtype)[None, :, None, :, None]]
where the time goes in v3:
time: 33.1 us; the launch traced here: 32.9 us
  Pallas kernels  32.9 us (99%)
    pallas_call x1, Pallas kernels, exchange_form(): pl.pallas_call(functools.partial(main_kernel, rows, cols), out_shape=jax....  29.6 us
    pallas_call x1, Pallas kernels, exchange_form(): pl.pallas_call(place_kernel, grid=(bands, 2), in_specs=[pl.BlockSpec((chu...  3.33 us

profile of v3, /device:TPU:25, one launch (start us, length us, event | category | flops | bytes accessed | tf_op | source)
XLA Modules:
  0.0 32.9 jit_solution(2609249791974670985)
XLA Ops:
  0.0 29.6 %shard_map.28.x_ref = bf16[16,8,16,128]{3,2,1,0:T(8,128)(2,1)} custom-call(bf16[2,32,2,2,1024]{4,3,2,1,0:T(2,128)(2,1)} %x_ref.1, s32[2,32]{1,0:T(2,128)} %bitcast.1), custom_call_target="tpu_custom_call" | custom-call | tf_op jit(solution)/shard_map/pallas_call | solution.py:332
  29.6 3.3 %shard_map.29 = f32[2,2,1,16,4,1024]{5,4,3,2,1,0:T(4,128)} custom-call(bf16[16,8,16,128]{3,2,1,0:T(8,128)(2,1)} %shard_map.28.x_ref), custom_call_target="tpu_custom_call" | custom-call | tf_op jit(solution)/shard_map/pallas_call | solution.py:354

commit v4 on v3

--- a/solution.py
+++ b/solution.py
@@ -171,8 +171,8 @@
 
 
 def main_kernel(
-    rows, cols, x_ref, flag_ref, got_ref, spread, sent, held, wide_ref, total_ref, pairs,
-    send_sem, recv_sem, own_sem, back_send, back_recv, back_own,
+    rows, cols, raw_ref, flag_ref, got_ref, x_ref, spread, sent, held, wide_ref, total_ref, pairs,
+    send_sem, recv_sem, own_sem, back_send, back_recv, back_own, in_sem,
 ):
     count = rows * cols
     windows = x_ref.shape[1]
@@ -185,6 +185,13 @@
         return {"row": peer // cols, "col": lax.rem(peer, cols)}
 
     barrier = pltpu.get_barrier_semaphore()
+    loads = []
+    for half in range(2):
+        part = pl.ds(half * part_windows, part_windows)
+        loads.append(
+            pltpu.make_async_copy(raw_ref.at[:, part], x_ref.at[:, part], in_sem.at[half])
+        )
+        loads[half].start()
     for k in range(1, count):
         pl.semaphore_signal(
             barrier,
@@ -194,6 +201,7 @@
         )
     copies, owns = [[], []], []
     for half in range(2):
+        loads[half].wait()
         whiten_windows(x_ref, flag_ref, spread, sent.at[half], half * part_windows, part_windows)
         if half == 0:
             pl.semaphore_wait(barrier, count - 1)
@@ -308,21 +316,35 @@
                     own_copy(k, n % cols).wait()
 
 
-def place_kernel(x_ref, o_ref):
+def place_kernel(bands, x_ref, o_ref, taken, placed, in_sem, out_sem):
     row, col = lax.axis_index("row"), lax.axis_index("col")
-    chunks, rows = x_ref.shape[:2]
+    chunks, rows = x_ref.shape[0] // bands, x_ref.shape[1]
+    loads = []
+    for b in range(bands):
+        here = pl.ds(b * chunks, chunks)
+        loads.append(pltpu.make_async_copy(x_ref.at[here], taken.at[here], in_sem.at[b]))
+        loads[-1].start()
     index = lax.broadcasted_iota(jnp.int32, (8, LANES), 0)
     second = row * 4 + lax.rem(index, 4)
-    for q in range(rows):
-        keep = q * 4 + col * 2 + index // 4 <= second
-        for c in range(chunks):
-            pair = x_ref[c, q].astype(jnp.float32)
-            for p in range(2):
-                value = jnp.where(keep, pair[p * 8 : p * 8 + 8], 0.0)
-                for k in range(2):
-                    o_ref[0, p, 0, q * 2 + k, :, c * LANES : (c + 1) * LANES] = value[
-                        k * 4 : k * 4 + 4
-                    ]
+    stores = []
+    for b in range(bands):
+        loads[b].wait()
+        for p in range(2):
+            for q in range(rows):
+                keep = q * 4 + col * 2 + index // 4 <= second
+                for c in range(chunks):
+                    pair = taken[b * chunks + c, q].astype(jnp.float32)
+                    value = jnp.where(keep, pair[p * 8 : p * 8 + 8], 0.0)
+                    for k in range(2):
+                        placed[b, p, 0, q * 2 + k, :, c * LANES : (c + 1) * LANES] = value[
+                            k * 4 : k * 4 + 4
+                        ]
+            stores.append(
+                pltpu.make_async_copy(placed.at[b, p], o_ref.at[b, p], out_sem.at[b, p])
+            )
+            stores[-1].start()
+    for store in stores:
+        store.wait()
 
 
 def exchange_form(rows, cols, spectra, window_flags):
@@ -332,9 +354,13 @@
     got = pl.pallas_call(
         functools.partial(main_kernel, rows, cols),
         out_shape=jax.ShapeDtypeStruct((count, rows, 16, LANES), jnp.bfloat16),
-        in_specs=[pl.BlockSpec(memory_space=pltpu.VMEM)] * 2,
+        in_specs=[
+            pl.BlockSpec(memory_space=pl.ANY),
+            pl.BlockSpec(memory_space=pltpu.VMEM),
+        ],
         out_specs=pl.BlockSpec(memory_space=pl.ANY),
         scratch_shapes=[
+            pltpu.VMEM(spectra.shape, spectra.dtype),
             pltpu.VMEM((bands, parts, bins // LANES, windows // 2 * chans, LANES), jnp.float32),
             pltpu.VMEM((2, count, height // 2, LANES), jnp.bfloat16),
             pltpu.VMEM((2, count, height // 2, LANES), jnp.bfloat16),
@@ -347,18 +373,22 @@
             pltpu.SemaphoreType.DMA((count,)),
             pltpu.SemaphoreType.DMA((count,)),
             pltpu.SemaphoreType.DMA,
+            pltpu.SemaphoreType.DMA((2,)),
         ],
         compiler_params=pltpu.CompilerParams(collective_id=0, has_side_effects=True),
     )(spectra, jnp.transpose(window_flags))
-    chunks = count // bands // 2
+    shape = (bands, 2, 1, rows * chans, cols * chans, bins)
     return pl.pallas_call(
-        place_kernel,
-        grid=(bands, 2),
-        in_specs=[pl.BlockSpec((chunks, rows, 16, LANES), lambda b, n: (b * 2 + n, 0, 0, 0))],
-        out_specs=pl.BlockSpec(
-            (1, 2, 1, rows * chans, cols * chans, bins // 2), lambda b, n: (b, 0, 0, 0, 0, n)
-        ),
-        out_shape=jax.ShapeDtypeStruct((bands, 2, 1, rows * chans, cols * chans, bins), jnp.float32),
+        functools.partial(place_kernel, bands),
+        in_specs=[pl.BlockSpec(memory_space=pl.ANY)],
+        out_specs=pl.BlockSpec(memory_space=pl.ANY),
+        out_shape=jax.ShapeDtypeStruct(shape, jnp.float32),
+        scratch_shapes=[
+            pltpu.VMEM(got.shape, got.dtype),
+            pltpu.VMEM(shape, jnp.float32),
+            pltpu.SemaphoreType.DMA((bands,)),
+            pltpu.SemaphoreType.DMA((bands, 2)),
+        ],
     )(got)
 
 

time: 33.1 us -> 31.4 us (0.949)
  Pallas kernels: 32.9 us -> 31.2 us
    pallas_call x1, Pallas kernels: 3.33 us -> 2 us  [exchange_form(): pl.pallas_call(functools.partial(place_kernel, bands), in_specs=[pl.Block...]
    pallas_call x1, Pallas kernels: 29.6 us -> 29.2 us  [exchange_form(): pl.pallas_call(functools.partial(main_kernel, rows, cols), out_shape=jax....]
where the time goes in v4:
time: 31.4 us; the launch traced here: 31.2 us
  Pallas kernels  31.2 us (99%)
    pallas_call x1, Pallas kernels, exchange_form(): pl.pallas_call(functools.partial(main_kernel, rows, cols), out_shape=jax....  29.2 us
    pallas_call x1, Pallas kernels, exchange_form(): pl.pallas_call(functools.partial(place_kernel, bands), in_specs=[pl.Block...  2 us

profile of v4, /device:TPU:25, one launch (start us, length us, event | category | flops | bytes accessed | tf_op | source)
XLA Modules:
  0.0 31.2 jit_solution(2053630628673443377)
XLA Ops:
  0.0 29.2 %shard_map.28.x_ref = bf16[16,8,16,128]{3,2,1,0:T(8,128)(2,1)} custom-call(bf16[2,32,2,2,1024]{4,3,2,1,0:T(2,128)(2,1)} %raw_ref.1, s32[2,32]{1,0:T(2,128)} %bitcast.1), custom_call_target="tpu_custom_call" | custom-call | tf_op jit(solution)/shard_map/pallas_call | solution.py:354
  29.2 2.0 %shard_map.29 = f32[2,2,1,16,4,1024]{5,4,3,2,1,0:T(4,128)} custom-call(bf16[16,8,16,128]{3,2,1,0:T(8,128)(2,1)} %shard_map.28.x_ref), custom_call_target="tpu_custom_call" | custom-call | tf_op jit(solution)/shard_map/pallas_call | solution.py:381

commit v5 on v4

--- a/solution.py
+++ b/solution.py
@@ -264,7 +264,7 @@
 
     @pl.loop(0, rows)
     def _(step):
-        r = lax.rem(row + rows // 2 + step, rows)
+        r = rows - 1 - step
 
         def keep(h, q, value):
             pairs[r * cols + h, q] = (total_ref[r * cols + h, q] + value).astype(jnp.bfloat16)

time: 31.4 us -> 31.8 us (1.013)
  the two profiles are of different devices: /device:TPU:25 before, /device:TPU:17 now
where the time goes in v5:
time: 31.8 us; the launch traced here: 31.6 us
  Pallas kernels  31.6 us (99%)
    pallas_call x1, Pallas kernels, exchange_form(): pl.pallas_call(functools.partial(main_kernel, rows, cols), out_shape=jax....  29.6 us
    pallas_call x1, Pallas kernels, exchange_form(): pl.pallas_call(functools.partial(place_kernel, bands), in_specs=[pl.Block...  2 us

profile of v5, /device:TPU:17, one launch (start us, length us, event | category | flops | bytes accessed | tf_op | source)
XLA Modules:
  0.0 31.6 jit_solution(5581119742929839675)
XLA Ops:
  0.0 29.6 %shard_map.28.x_ref = bf16[16,8,16,128]{3,2,1,0:T(8,128)(2,1)} custom-call(bf16[2,32,2,2,1024]{4,3,2,1,0:T(2,128)(2,1)} %raw_ref.1, s32[2,32]{1,0:T(2,128)} %bitcast.1), custom_call_target="tpu_custom_call" | custom-call | tf_op jit(solution)/shard_map/pallas_call | solution.py:354
  29.6 2.0 %shard_map.29 = f32[2,2,1,16,4,1024]{5,4,3,2,1,0:T(4,128)} custom-call(bf16[16,8,16,128]{3,2,1,0:T(8,128)(2,1)} %shard_map.28.x_ref), custom_call_target="tpu_custom_call" | custom-call | tf_op jit(solution)/shard_map/pallas_call | solution.py:381
